TPU v7x, 512 devices: a whole 4x4x16 slice. The times are simulated.
512 devices in a mesh: cell: 32 (over z_lo, x, core), feat: 16 (over z_hi, y).
Axes of the slice: x: 4, y: 4, z: 16 (z_hi: 4, z_lo: 4; z = z_hi * 4 + z_lo), core: 2. Of those that a mesh axis runs over, the one named last changes fastest.
Arguments:
- rna_counts: bfloat16 [65536, 4096], P('cell', 'feat'), may hold values from -6 to 6
- rna_embed: bfloat16 [65536, 64], P('cell'), may hold values from -3 to 3
- rna_potential: float32 [65536], P('cell'), may hold values from -1 to 1
- atac_counts: bfloat16 [16384, 16384], P('feat', 'cell'), may hold values from -6 to 6
- atac_embed: bfloat16 [16384, 64], P('feat'), may hold values from -3 to 3
- atac_potential: bfloat16 [16384], P('feat'), may hold values from -1 to 1
- panel_ids: int32 [1024], P('feat'), may hold values from 0 to 16383, as said below
Outputs:
- feature_cross: bfloat16 [4096, 16384], P('feat', 'cell')
- gene_term: float32 [4096], P('feat')
- peak_term: float32 [16384], P('cell')
Inputs may be any that keep to these rules, and one draw needn't show every extreme that they name: `panel_ids`: the ids in slots k * 64 to (k + 1) * 64 - 1 are distinct and lie among ATAC cells k * 1024 to (k + 1) * 1024 - 1.
All inputs are finite; a program needn't handle non-finite values.
Results may differ from a plain program's by a relative error of at most 0.0058.
Values may be sent and summed in bfloat16 or wider, within the bound.
A program may use at most 64 MiB of HBM per device.

v0:
```python
import math
import jax
import jax.numpy as jnp
from jax import lax
from jax.sharding import PartitionSpec as P


def local(rna_counts, rna_embed, rna_potential, atac_counts, atac_embed, atac_potential, panel_ids):
    owner = lax.axis_index("feat")
    local_ids = panel_ids - owner * atac_counts.shape[0]
    chosen_rows = jnp.take(atac_counts, local_ids, axis=0)
    chosen_embed = jnp.take(atac_embed, local_ids, axis=0)
    chosen_potential = jnp.take(atac_potential, local_ids, axis=0)
    panel_rows, panel_embed, panel_potential = (
        lax.all_gather(chosen_rows, "feat", axis=0, tiled=True),
        lax.all_gather(chosen_embed, "feat", axis=0, tiled=True),
        lax.all_gather(chosen_potential, "feat", axis=0, tiled=True),
    )
    panel_float = panel_potential.astype(jnp.float32)
    inverse = 1.0 / math.sqrt(rna_embed.shape[1])
    rows_here = rna_counts.shape[0]
    genes_here = rna_counts.shape[1]
    panel_size = panel_embed.shape[0]
    height = min(512, rows_here)
    number = rows_here // height
    items = (
        rna_counts.reshape(number, height, genes_here),
        rna_embed.reshape(number, height, rna_embed.shape[1]),
        rna_potential.reshape(number, height),
    )

    def advance(carry, item):
        total, gene_sum, panel_mass = carry
        block_rows, block_embed, block_potential = item
        score = lax.dot_general(
            block_embed, panel_embed, (((1,), (1,)), ((), ())), preferred_element_type=jnp.float32
        )
        coupling = jnp.exp(
            block_potential[:, None] + panel_float[None, :] + score * inverse
        ).astype(jnp.bfloat16)
        widened = coupling.astype(jnp.float32)
        row_mass = jnp.sum(widened, axis=1)
        panel_mass = panel_mass + jnp.sum(widened, axis=0)
        total = total + lax.dot_general(
            block_rows, coupling, (((0,), (0,)), ((), ())), preferred_element_type=jnp.float32
        )
        squares = jnp.square(block_rows.astype(jnp.float32))
        gene_sum = gene_sum + jnp.dot(row_mass, squares, precision=lax.Precision.HIGHEST)
        return ((total, gene_sum, panel_mass), None)

    start = (
        jnp.zeros((genes_here, panel_size), jnp.float32),
        jnp.zeros((genes_here,), jnp.float32),
        jnp.zeros((panel_size,), jnp.float32),
    )
    (total, gene_sum, panel_mass), unused = lax.scan(advance, start, items)
    total, gene_sum, panel_mass = lax.psum((total, gene_sum, panel_mass), "cell")
    reduced = total.astype(jnp.bfloat16)
    all_rows = rows_here * lax.axis_size("cell")
    scale = 1.0 / math.sqrt(all_rows * panel_size)
    mass_scale = 1.0 / (all_rows * panel_size)
    feature_cross = (
        jnp.dot(reduced, panel_rows, preferred_element_type=jnp.float32) * scale
    ).astype(jnp.bfloat16)
    gene_term = gene_sum * mass_scale
    peak_term = (
        jnp.dot(
            panel_mass, jnp.square(panel_rows.astype(jnp.float32)), precision=lax.Precision.HIGHEST
        )
        * mass_scale
    )
    return (feature_cross, gene_term, peak_term)


def solution(mesh):
    placed = (
        P("cell", "feat"),
        P("cell", None),
        P("cell"),
        P("feat", "cell"),
        P("feat", None),
        P("feat"),
        P("feat"),
    )
    return jax.shard_map(
        local,
        mesh=mesh,
        in_specs=placed,
        out_specs=(P("feat", "cell"), P("feat"), P("cell")),
        check_vma=False,
    )
```

profile of v0, /device:TPU:8, one launch (start us, length us, event | category | flops | bytes accessed | tf_op | source)
XLA Modules:
  0.0 298.3 jit_solution(12561693052006271583)
XLA Ops:
  7.2 0.0 all-gather.2.cloned.1.call-start
  7.3 0.7 compare_and_fusion
  8.0 0.4 copy-done
  8.4 0.7 gather_fusion.2
  9.1 0.7 broadcast_select_fusion
  9.9 0.8 gather_fusion
  10.7 1.3 dynamic-slice
  12.6 0.2 dynamic-update-slice
  12.9 52.7 %all-reduce = bf16[1024]{0:T(1024)(128)(2,1)S(1)} all-reduce(bf16[1024]{0:T(1024)(128)(2,1)S(1)} %dynamic-update-slice), channel_id=1, replica_groups=mesh['cell'=32,'feat'=16] {'feat'}, use_global_device_ids=true, to_apply=%add | all-reduce | flops 1024 | bytes 4096
  65.6 0.2 copy.13
  65.7 0.6 gather_fusion.1
  66.4 0.1 broadcast_select_fusion.1
  66.5 54.9 %all_gather.10 = bf16[1024,64]{1,0:T(8,128)(2,1)S(1)} all-gather(bf16[64,64]{1,0:T(8,128)(2,1)S(1)} %broadcast_select_fusion.1), channel_id=1, replica_groups=mesh['cell'=32,'feat'=16] {'feat'}, dimensions={0}, use_global_device_ids=true | all-gather | bytes 139264 | tf_op jit(solution)/shard_map/all_gather | solution.py:16
  121.3 1.0 copy.12
  122.4 18.1 %while.15 = (s32[]{:T(128)}, f32[256,1024]{1,0:T(8,128)S(1)}, f32[256]{0:T(256)S(1)}, f32[1024]{0:T(1024)S(1)}, bf16[4,512,256]{2,1,0:T(8,128)(2,1)}, /*index=5*...) while((s32[]{:T(128)}, f32[256,1024]{1,0:T(8,128)S(1)}, ...), condition=%wide.region_3.4_spmd.clone, body=%wide.region_0.3_spmd.clone.sunk | while | flops 341574656 | bytes 5017213 | solution.py:56
  122.4 1.7 convert_reduce_fusion.3
  124.0 1.5 convolution_add_fusion.2
  125.5 1.3 fusion.34
  126.9 1.7 convert_reduce_fusion.3
  128.6 1.5 convolution_add_fusion.2
  130.1 1.3 fusion.34
  131.4 1.7 convert_reduce_fusion.3
  133.1 1.5 convolution_add_fusion.2
  134.6 1.3 fusion.34
  136.0 1.7 convert_reduce_fusion.3
  137.6 1.5 convolution_add_fusion.2
  139.1 1.3 fusion.34
  140.5 146.1 %all-reduce.3 = (bf16[256,1024]{1,0:T(8,128)(2,1)S(1)}, f32[256]{0:T(256)S(1)}, f32[1024]{0:T(1024)S(1)}) all-reduce(f32[256,1024]{1,0:T(8,128)S(1)} %get-tuple-element.52, f32[256]{0:T(256)S(1)} %get-tuple-element.53, f32[1024]{0:T(1024)S(1)} %get-tuple-element.54), channel_id=1, replica_groups=mesh['cell'=32,'feat'=16] {'cell'}, use_global_device_ids=true, to_apply=%region_4.5 | all-reduce | flops 263424 | bytes 1583104 | tf_op jit(solution)/shard_map/psum | solution.py:57
  286.6 0.6 broadcast_multiply_fusion.1
  287.2 2.5 fusion.12
  289.7 0.6 broadcast_multiply_fusion
  290.3 1.1 fusion.15
  (33 shorter events, 0.3 us)
Async XLA Ops:
  7.2 1.2 copy-start
  7.2 2.7 copy-start.1
  7.2 58.4 %copy-start.4 = (bf16[1024,64]{0,1:T(8,128)(2,1)S(1)}, bf16[1024,64]{0,1:T(8,128)(2,1)}, u32[]{:S(2)}) copy-start(bf16[1024,64]{0,1:T(8,128)(2,1)} %param.13) | copy-start | bytes 393220
  7.2 280.0 %all-gather.2.cloned.1.call-start = ((), (), s32[]{:S(2)}) async-start(), calls=%async_computation | async-start | bytes 1114112 | tf_op jit(solution)/shard_map/all_gather | solution.py:15
  8.4 112.9 %copy-start.3 = (bf16[2048,64]{0,1:T(8,128)(2,1)S(1)}, bf16[2048,64]{0,1:T(8,128)(2,1)}, u32[]{:S(2)}) copy-start(bf16[2048,64]{0,1:T(8,128)(2,1)} %param.10) | copy-start | bytes 786436
  9.9 112.5 %copy-start.5 = (f32[2048]{0:T(1024)S(1)}, f32[2048]{0:T(1024)}, u32[]{:S(2)}) copy-start(f32[2048]{0:T(1024)} %param.11) | copy-start | bytes 24580
  287.2 3.1 %copy-start.2 = (bf16[1024,512]{1,0:T(8,128)(2,1)S(1)}, bf16[1024,512]{1,0:T(8,128)(2,1)}, u32[]{:S(2)}) copy-start(bf16[1024,512]{1,0:T(8,128)(2,1)} %all-gather.2.cloned.1.call-done) | copy-start | bytes 3145732
Sparse Core Ops, SparseCore 0:
  11.6 81.7 all-gather.1
where the time goes:
time: 299 us; the launch traced here: 298 us
  blocking collectives  254 us (85%)
  matrix products  21.4 us (7%)
  between operations  14.8 us (5%)
  local copies, waits for them, and re-layouts  5.31 us (2%)
    psum x1, blocking collectives, local(): lax.psum((total, gene_sum, panel_mass), 'cell')  146 us
    all_gather x1, blocking collectives, local(): lax.all_gather(chosen_embed, 'feat', axis=0, tiled=True)  54.9 us
    unnamed x1, blocking collectives  52.7 us
    dot_general x4, matrix products, advance(): lax.dot_general(block_embed, panel_embed, (((1,), (1,)), ((), ())), prefe...  6.7 us
  transfers between devices with their start and end apart: 1, of which 0 were waited for; matrix products, arithmetic and copies ran while one was open for 8% of the time, Pallas kernels for 0%

commit v1 on v0

--- a/solution.py
+++ b/solution.py
@@ -13,7 +13,9 @@
     chosen_potential = jnp.take(atac_potential, local_ids, axis=0)
     panel_rows, panel_embed, panel_potential = (
         lax.all_gather(chosen_rows, "feat", axis=0, tiled=True),
-        lax.all_gather(chosen_embed, "feat", axis=0, tiled=True),
+        jnp.concatenate(
+            lax.all_to_all(jnp.stack([chosen_embed] * lax.axis_size("feat")), "feat", 0, 0), axis=0
+        ),
         lax.all_gather(chosen_potential, "feat", axis=0, tiled=True),
     )
     panel_float = panel_potential.astype(jnp.float32)

time: 299 us -> 260 us (0.87)
  blocking collectives: 254 us -> 195 us
  starting transfers between devices: 0.04 us -> 18.2 us
    all_gather x1 -> x0, blocking collectives: 54.9 us -> none  [local(): lax.all_gather(chosen_embed, 'feat', axis=0, tiled=True)]
    all_to_all x0 -> x1, starting transfers between devices: none -> 18.2 us  [local(): lax.all_to_all(jnp.stack([chosen_embed] * lax.axis_size('feat')), 'feat',...]
    unnamed x1, blocking collectives: 52.7 us -> 47.2 us
  transfers between devices with their start and end apart: 1 -> 2, of which waited for: 0 -> 0; matrix products, arithmetic and copies ran while one was open for 8% -> 9% of each run, Pallas kernels for 0% -> 0%
where the time goes in v1:
time: 260 us; the launch traced here: 259 us
  blocking collectives  195 us (75%)
  matrix products  21.4 us (8%)
  starting transfers between devices  18.2 us (7%)
  between operations  14.8 us (6%)
  local copies, waits for them, and re-layouts  6.95 us (3%)
  other arithmetic  2.91 us (1%)
    psum x1, blocking collectives, local(): lax.psum((total, gene_sum, panel_mass), 'cell')  148 us
    unnamed x1, blocking collectives  47.2 us
    all_to_all x1, starting transfers between devices, local(): lax.all_to_all(jnp.stack([chosen_embed] * lax.axis_size('feat')), 'feat',...  18.2 us
    dot_general x4, matrix products, advance(): lax.dot_general(block_embed, panel_embed, (((1,), (1,)), ((), ())), prefe...  6.7 us
    dot_general x4, matrix products, advance(): lax.dot_general(block_rows, coupling, (((0,), (0,)), ((), ())), preferred...  5.96 us
  transfers between devices with their start and end apart: 2, of which 0 were waited for; matrix products, arithmetic and copies ran while one was open for 9% of the time, Pallas kernels for 0%

profile of v1, /device:TPU:8, one launch (start us, length us, event | category | flops | bytes accessed | tf_op | source)
XLA Modules:
  0.0 259.2 jit_solution(2083175445968312489)
XLA Ops:
  7.2 0.8 compare_and_fusion
  7.9 1.1 copy.13
  9.0 0.6 gather_fusion.1
  9.7 0.1 broadcast_select_fusion.1
  9.8 0.9 reshape.74
  10.7 18.2 %all-to-all-start = ((bf16[16,2,2048]{2,1,0:T(2,128)(2,1)}), bf16[16,2,2048]{2,1,0:T(2,128)(2,1)S(1)}, u32[]{:S(2)}, u32[]{:S(2)}) async-start(bf16[16,2,2048]{2,1,0:T(2,128)(2,1)} %reshape.74), calls=%async_computation | async-start | bytes 262144 | tf_op jit(solution)/shard_map/all_to_all | solution.py:17
  29.0 0.7 gather_fusion.2
  29.7 0.7 broadcast_select_fusion
  30.4 0.8 gather_fusion
  31.2 1.3 dynamic-slice
  33.2 0.2 dynamic-update-slice
  33.4 47.2 %all-reduce = bf16[1024]{0:T(1024)(128)(2,1)S(1)} all-reduce(bf16[1024]{0:T(1024)(128)(2,1)S(1)} %dynamic-update-slice), channel_id=1, replica_groups=mesh['cell'=32,'feat'=16] {'feat'}, use_global_device_ids=true, to_apply=%add | all-reduce | flops 1024 | bytes 4096
  80.6 1.0 copy.12
  81.6 0.2 reshape.75
  81.8 18.1 %while.15 = (s32[]{:T(128)}, f32[256,1024]{1,0:T(8,128)S(1)}, f32[256]{0:T(256)S(1)}, f32[1024]{0:T(1024)S(1)}, bf16[4,512,256]{2,1,0:T(8,128)(2,1)}, /*index=5*...) while((s32[]{:T(128)}, f32[256,1024]{1,0:T(8,128)S(1)}, ...), condition=%wide.region_3.4_spmd.clone, body=%wide.region_0.3_spmd.clone.sunk | while | flops 341574656 | bytes 5017213 | solution.py:58
  81.9 1.7 convert_reduce_fusion.3
  83.6 1.5 convolution_add_fusion.2
  85.0 1.3 fusion.34
  86.4 1.7 convert_reduce_fusion.3
  88.1 1.5 convolution_add_fusion.2
  89.6 1.3 fusion.34
  90.9 1.7 convert_reduce_fusion.3
  92.6 1.5 convolution_add_fusion.2
  94.1 1.3 fusion.34
  95.5 1.7 convert_reduce_fusion.3
  97.2 1.5 convolution_add_fusion.2
  98.7 1.3 fusion.34
  100.0 147.5 %all-reduce.3 = (bf16[256,1024]{1,0:T(8,128)(2,1)S(1)}, f32[256]{0:T(256)S(1)}, f32[1024]{0:T(1024)S(1)}) all-reduce(f32[256,1024]{1,0:T(8,128)S(1)} %get-tuple-element.52, f32[256]{0:T(256)S(1)} %get-tuple-element.53, f32[1024]{0:T(1024)S(1)} %get-tuple-element.54), channel_id=1, replica_groups=mesh['cell'=32,'feat'=16] {'cell'}, use_global_device_ids=true, to_apply=%region_4.5 | all-reduce | flops 263424 | bytes 1583104 | tf_op jit(solution)/shard_map/psum | solution.py:59
  247.5 0.6 broadcast_multiply_fusion.1
  248.1 2.5 fusion.12
  250.6 0.6 broadcast_multiply_fusion
  251.2 1.1 fusion.15
  (35 shorter events, 0.4 us)
Async XLA Ops:
  7.2 21.8 %copy-start = (bf16[1024,512]{1,0:T(8,128)(2,1)S(1)}, bf16[1024,512]{1,0:T(8,128)(2,1)}, u32[]{:S(2)}) copy-start(bf16[1024,512]{1,0:T(8,128)(2,1)} %param.12) | copy-start | bytes 3145732
  9.0 21.4 %copy-start.1 = (bf16[1024]{0:T(1024)(128)(2,1)S(1)}, bf16[1024]{0:T(1024)(128)(2,1)}, u32[]{:S(2)}) copy-start(bf16[1024]{0:T(1024)(128)(2,1)} %param.14) | copy-start | bytes 6148
  9.8 70.8 %copy-start.3 = (bf16[2048,64]{0,1:T(8,128)(2,1)S(1)}, bf16[2048,64]{0,1:T(8,128)(2,1)}, u32[]{:S(2)}) copy-start(bf16[2048,64]{0,1:T(8,128)(2,1)} %param.10) | copy-start | bytes 786436
  10.7 70.9 %all-to-all-start = ((bf16[16,2,2048]{2,1,0:T(2,128)(2,1)}), bf16[16,2,2048]{2,1,0:T(2,128)(2,1)S(1)}, u32[]{:S(2)}, u32[]{:S(2)}) async-start(bf16[16,2,2048]{2,1,0:T(2,128)(2,1)} %reshape.74), calls=%async_computation | async-start | bytes 262144 | tf_op jit(solution)/shard_map/all_to_all | solution.py:17
  28.9 52.7 %copy-start.4 = (f32[2048]{0:T(1024)S(1)}, f32[2048]{0:T(1024)}, u32[]{:S(2)}) copy-start(f32[2048]{0:T(1024)} %param.11) | copy-start | bytes 24580
  28.9 219.2 %all-gather.2.cloned.1.call-start = ((), (), s32[]{:S(2)}) async-start(), calls=%async_computation.1 | async-start | bytes 1114112 | tf_op jit(solution)/shard_map/all_gather | solution.py:15
  248.1 3.1 %copy-start.2 = (bf16[1024,512]{1,0:T(8,128)(2,1)S(1)}, bf16[1024,512]{1,0:T(8,128)(2,1)}, u32[]{:S(2)}) copy-start(bf16[1024,512]{1,0:T(8,128)(2,1)} %all-gather.2.cloned.1.call-done) | copy-start | bytes 3145732
Sparse Core Ops, SparseCore 0:
  32.7 78.3 all-gather.1
